TPU v7x, 32 devices: a whole 2x2x4 slice. The times are simulated.
32 devices in a mesh: ctx: 8 (over z, x), exp: 4 (over y, core).
Axes of the slice: x: 2, y: 2, z: 4, core: 2. Of those that a mesh axis runs over, the one named last changes fastest.
Arguments:
- hidden_states: bfloat16 [4096, 4096], P(('ctx', 'exp')), may hold values from -70 to 70
- upstream: bfloat16 [4096, 4096], P(('ctx', 'exp')), may hold values from -6 to 6
- norm_gain: float32 [4096], replicated, may hold values from 0.5 to 1.5
- router: bfloat16 [4096, 8], replicated, may hold values from -4 to 4
- expert_ids: int32 [4096, 8], P(('ctx', 'exp')), may hold values from 0 to 7, as said below
- w_gate: bfloat16 [8, 4096, 1536], P('ctx', None, 'exp'), may hold values from -0.09375 to 0.09375
- w_up: bfloat16 [8, 4096, 1536], P('ctx', None, 'exp'), may hold values from -0.09375 to 0.09375
- w_down: bfloat16 [8, 1536, 4096], P('ctx', 'exp'), may hold values from -0.15625 to 0.15625
Outputs:
- grad_input: bfloat16 [4096, 4096], P(('ctx', 'exp'))
Inputs may be any that keep to these rules, and one draw needn't show every extreme that they name: `expert_ids`: A token's 8 entries differ. Among the rows of one device, no expert is named in column 0 by more than 24 rows, and in every device's rows one expert is named there by exactly 24.
All inputs are finite; a program needn't handle non-finite values.
Results may differ from a plain program's by a relative error of at most 0.012.
Values may be sent and summed in bfloat16 or wider, within the bound.
A program may use at most 128 MiB of HBM per device.

v0:
```python
import jax
import jax.numpy as jnp
from jax import lax
from jax.sharding import PartitionSpec as P

EPSILON = 1e-06


def silu_parts(pre_value):
    sigmoid_value = jax.nn.sigmoid(pre_value)
    return (pre_value * sigmoid_value, sigmoid_value * (1.0 + pre_value * (1.0 - sigmoid_value)))


def dispatch(stacked, experts, capacity, model_width):
    layers = stacked.shape[0]
    shaped = stacked.reshape(layers, experts, capacity, model_width)
    moved = lax.all_to_all(shaped, "ctx", split_axis=1, concat_axis=1, tiled=True)
    grouped = lax.all_gather(moved, "exp", axis=1, tiled=True)
    return grouped.reshape(layers, -1, model_width)


def place(values, target, slot_total):
    empty = jnp.zeros((values.shape[0], slot_total, values.shape[2]), values.dtype)
    return empty.at[:, target, :].set(values)


def per_device(hidden_states, upstream, norm_gain, router, expert_ids, w_gate, w_up, w_down):
    tok_rows, model_width = hidden_states.shape
    experts = router.shape[1]
    capacity = 3 * tok_rows // (2 * experts)
    slot_total = experts * capacity
    widened = hidden_states.astype(jnp.float32)
    inverse = lax.rsqrt(jnp.mean(widened * widened, axis=1, keepdims=True) + EPSILON)
    normed = (widened * inverse * norm_gain).astype(jnp.bfloat16)
    logits = jnp.dot(normed, router, preferred_element_type=jnp.float32)
    probability = jax.nn.softmax(logits, axis=1)
    labels = jnp.arange(experts, dtype=jnp.int32)
    chosen = (expert_ids[:, :, None] == labels).astype(jnp.float32)
    primary = chosen[:, 0, :]
    member = jnp.sum(chosen, axis=1)
    top_prob = jnp.sum(probability * primary, axis=1)
    route_mass = jnp.sum(probability * member, axis=1)
    gate_value = top_prob / route_mass
    upstream_wide = upstream.astype(jnp.float32)
    scaled_grad = (gate_value[:, None] * upstream_wide).astype(jnp.bfloat16)
    before = jnp.cumsum(primary, axis=0) - primary
    slot_index = jnp.sum(before * primary, axis=1).astype(jnp.int32)
    target = expert_ids[:, 0] * capacity + slot_index
    expert_rows = dispatch(place(normed[None], target, slot_total), experts, capacity, model_width)[
        0
    ]
    gate_block = w_gate[0]
    up_block = w_up[0]
    down_block = w_down[0]
    pre_gate = jnp.dot(expert_rows, gate_block, preferred_element_type=jnp.float32)
    pre_up = jnp.dot(expert_rows, up_block, preferred_element_type=jnp.float32)
    activated, act_slope = silu_parts(pre_gate)
    hidden = (activated * pre_up).astype(jnp.bfloat16)
    summed = lax.psum_scatter(
        jnp.dot(hidden, down_block, preferred_element_type=jnp.float32).astype(jnp.bfloat16),
        "exp",
        scatter_dimension=0,
        tiled=True,
    )
    outgoing = summed.reshape(experts, capacity, model_width)
    returned = lax.all_to_all(outgoing, "ctx", split_axis=0, concat_axis=0, tiled=True).reshape(
        slot_total, model_width
    )
    expert_out = returned[target].astype(jnp.float32)
    grad_rows = dispatch(
        place(scaled_grad[None], target, slot_total), experts, capacity, model_width
    )[0]
    hidden_grad = lax.dot_general(
        grad_rows, down_block, (((1,), (1,)), ((), ())), preferred_element_type=jnp.float32
    )
    grad_pre_gate = (hidden_grad * pre_up * act_slope).astype(jnp.bfloat16)
    grad_pre_up = (hidden_grad * activated).astype(jnp.bfloat16)
    gate_part = lax.dot_general(
        grad_pre_gate, gate_block, (((1,), (1,)), ((), ())), preferred_element_type=jnp.float32
    )
    up_part = lax.dot_general(
        grad_pre_up, up_block, (((1,), (1,)), ((), ())), preferred_element_type=jnp.float32
    )
    grad_summed = lax.psum_scatter(
        (gate_part + up_part).astype(jnp.bfloat16), "exp", scatter_dimension=0, tiled=True
    )
    grad_outgoing = grad_summed.reshape(experts, capacity, model_width)
    grad_returned = lax.all_to_all(
        grad_outgoing, "ctx", split_axis=0, concat_axis=0, tiled=True
    ).reshape(slot_total, model_width)
    expert_grad = grad_returned[target].astype(jnp.float32)
    gate_grad = jnp.sum(upstream_wide * expert_out, axis=1)
    prob_grad = gate_grad[:, None] * (
        primary / route_mass[:, None] - (top_prob / (route_mass * route_mass))[:, None] * member
    )
    logit_grad = probability * (prob_grad - jnp.sum(probability * prob_grad, axis=1, keepdims=True))
    normed_grad = expert_grad + jnp.dot(
        logit_grad, router.astype(jnp.float32).T, precision=lax.Precision.HIGHEST
    )
    scaled = normed_grad * norm_gain
    grad_input = (
        inverse * scaled
        - widened * inverse**3 * jnp.sum(scaled * widened, axis=1, keepdims=True) / model_width
    )
    return grad_input.astype(jnp.bfloat16)


def solution(mesh):
    placed = (
        P(("ctx", "exp"), None),
        P(("ctx", "exp"), None),
        P(),
        P(),
        P(("ctx", "exp"), None),
        P("ctx", None, "exp"),
        P("ctx", None, "exp"),
        P("ctx", "exp", None),
    )
    return jax.shard_map(
        per_device, mesh=mesh, in_specs=placed, out_specs=P(("ctx", "exp"), None), check_vma=False
    )
```

profile of v0, /device:TPU:0, one launch (start us, length us, event | category | flops | bytes accessed | tf_op | source)
XLA Modules:
  0.0 332.9 jit_solution(14029999209317259293)
XLA Ops:
  8.2 1.5 fusion.13
  10.1 1.7 fusion.47
  12.6 4.2 %scatter_custom_fusion.1 = bf16[192,4096]{1,0:T(8,128)(2,1)} fusion(s32[128]{0:T(128)S(1)} %fusion.42, bf16[]{:T(256)} %constant.4.clone.1, bf16[128,4096]{1,0:T(8,128)(2,1)} %param.8, f32[4096]{0:T(1024)S(1)} %copy-done.12, f32[128]{0:T(128)S(1)} %get-tuple-element.11), kind=kCustom, calls=%fused_computation.41 | custom fusion | flops 2097152 | bytes 2638338 | tf_op jit(solution)/shard_map/scatter | solution.py:24
  16.7 44.4 %all_to_all.20 = bf16[1,8,24,4096]{3,2,0,1:T(8,128)(2,1)} all-to-all(bf16[1,8,24,4096]{3,2,0,1:T(8,128)(2,1)} %bitcast.54), channel_id=1, replica_groups=mesh['ctx'=8,'exp'=4] {'ctx'}, dimensions={1} | all-to-all | bytes 3145728 | tf_op jit(solution)/shard_map/all_to_all | solution.py:17
  61.2 4.1 %scatter_custom_fusion = bf16[192,4096]{1,0:T(8,128)(2,1)} fusion(s32[128]{0:T(128)S(1)} %fusion.42, bf16[128,4096]{1,0:T(8,128)(2,1)} %param.9, f32[128]{0:T(128)S(1)} %get-tuple-element.9, bf16[]{:T(256)} %constant.4.clone.1), kind=kCustom, calls=%fused_computation.39 | custom fusion | flops 1572864 | bytes 2621954 | tf_op jit(solution)/shard_map/scatter | solution.py:24
  65.3 40.5 %all_to_all.21 = bf16[1,8,24,4096]{3,2,0,1:T(8,128)(2,1)} all-to-all(bf16[1,8,24,4096]{3,2,0,1:T(8,128)(2,1)} %bitcast.53), channel_id=1, replica_groups=mesh['ctx'=8,'exp'=4] {'ctx'}, dimensions={1} | all-to-all | bytes 3145728 | tf_op jit(solution)/shard_map/all_to_all | solution.py:17
  106.7 6.6 %fusion.3 = f32[768,384]{1,0:T(8,128)S(1)} fusion(bf16[768,4096]{1,0:T(8,128)(2,1)} %bitcast.57, bf16[1,4096,384]{2,1,0:T(8,128)(2,1)} %param.13), kind=kOutput, calls=%fused_computation.14 | convolution fusion | flops 2415919104 | bytes 10616832 | tf_op jit(solution)/shard_map/dot_general | solution.py:55
  113.3 3.4 %fusion.6 = f32[768,384]{1,0:T(8,128)S(1)} fusion(bf16[768,4096]{1,0:T(8,128)(2,1)S(1)} %bitcast.58, bf16[1,4096,384]{2,1,0:T(8,128)(2,1)S(1)} %copy-done.8), kind=kOutput, calls=%fused_computation.17 | convolution fusion | flops 2415919104 | bytes 10616832 | tf_op jit(solution)/shard_map/dot_general | solution.py:56
  117.7 5.3 %convolution_convert_fusion = bf16[768,4096]{1,0:T(8,128)(2,1)} fusion(bf16[1,384,4096]{2,1,0:T(8,128)(2,1)S(1)} %copy-done, f32[768,384]{1,0:T(8,128)S(1)} %fusion.6, f32[768,384]{1,0:T(8,128)S(1)} %fusion.3), kind=kOutput, calls=%fused_computation.5 | convolution fusion | flops 2420834304 | bytes 11796480 | tf_op jit(solution)/shard_map/dot_general | solution.py:60
  123.3 31.4 %all-gather.3.cloned.1.call-done = bf16[1,32,24,4096]{3,2,0,1:T(8,128)(2,1)} async-done(((bf16[1,8,24,4096]{3,2,0,1:T(8,128)(2,1)}), bf16[1,32,24,4096]{3,2,0,1:T(8,128)(2,1)}) %all-gather.3.cloned.1.call-update) | async-done | bytes 6291472 | tf_op jit(solution)/shard_map/all_gather | solution.py:18
  154.7 5.7 %fusion.9 = f32[768,384]{1,0:T(8,128)S(1)} fusion(bf16[768,4096]{1,0:T(8,128)(2,1)} %bitcast.59, bf16[1,384,4096]{2,1,0:T(8,128)(2,1)S(1)} %copy-done), kind=kOutput, calls=%fused_computation.20 | convolution fusion | flops 2415919104 | bytes 10616832 | tf_op jit(solution)/shard_map/dot_general | solution.py:73
  160.4 1.0 copy-done.6
  161.4 3.6 %fusion.1 = f32[768,4096]{1,0:T(8,128)S(1)} fusion(bf16[1,4096,384]{2,1,0:T(8,128)(2,1)S(1)} %copy-done.7, f32[768,384]{1,0:T(8,128)S(1)} %copy-done.5, f32[768,384]{1,0:T(8,128)S(1)} %fusion.9, f32[768,384]{1,0:T(8,128)S(1)} %copy-done.10), kind=kOutput, calls=%fused_computation.12 | convolution fusion | flops 2418868224 | bytes 19267584 | tf_op jit(solution)/shard_map/dot_general | solution.py:78
  164.9 10.1 %add_convert_fusion = bf16[768,4096]{1,0:T(8,128)(2,1)} fusion(f32[768,4096]{1,0:T(8,128)S(1)} %fusion.1, bf16[1,4096,384]{2,1,0:T(8,128)(2,1)} %param.14, f32[768,384]{1,0:T(8,128)} %copy-done.6, f32[768,384]{1,0:T(8,128)} %copy-done.4), kind=kOutput, calls=%fused_computation.4 | convolution fusion | flops 2423980032 | bytes 24379392 | tf_op jit(solution)/shard_map/dot_general | solution.py:81
  175.1 40.5 %reduce-scatter.5.cloned.1.call-done = bf16[192,4096]{1,0:T(8,128)(2,1)} async-done(((bf16[768,4096]{1,0:T(8,128)(2,1)}), bf16[192,4096]{1,0:T(8,128)(2,1)}) %reduce-scatter.5.cloned.1.call-update) | async-done | bytes 1572880 | tf_op jit(solution)/shard_map/reduce_scatter | solution.py:59
  215.6 5.5 %all-to-all-start.3 = ((bf16[8,24,4096]{2,1,0:T(8,128)(2,1)}), bf16[8,24,4096]{2,1,0:T(8,128)(2,1)S(1)}, u32[]{:S(2)}, u32[]{:S(2)}) async-start(bf16[8,24,4096]{2,1,0:T(8,128)(2,1)} %bitcast.55), calls=%async_computation.5 | async-start | bytes 3145728 | tf_op jit(solution)/shard_map/all_to_all | solution.py:66
  221.1 55.4 %reduce-scatter.3.cloned.1.call-done = bf16[192,4096]{1,0:T(8,128)(2,1)} async-done(((bf16[768,4096]{1,0:T(8,128)(2,1)}), bf16[192,4096]{1,0:T(8,128)(2,1)}) %reduce-scatter.3.cloned.1.call-update) | async-done | bytes 1572880 | tf_op jit(solution)/shard_map/reduce_scatter | solution.py:84
  276.5 5.5 %all-to-all-start.2 = ((bf16[8,24,4096]{2,1,0:T(8,128)(2,1)}), bf16[8,24,4096]{2,1,0:T(8,128)(2,1)S(1)}, u32[]{:S(2)}, u32[]{:S(2)}) async-start(bf16[8,24,4096]{2,1,0:T(8,128)(2,1)} %bitcast.56), calls=%async_computation.3 | async-start | bytes 3145728 | tf_op jit(solution)/shard_map/all_to_all | solution.py:88
  282.1 2.2 gather_fusion.1
  284.2 1.9 fusion.12
  286.1 32.9 %all-to-all-done.2 = bf16[8,24,4096]{2,1,0:T(8,128)(2,1)S(1)} async-done(((bf16[8,24,4096]{2,1,0:T(8,128)(2,1)}), bf16[8,24,4096]{2,1,0:T(8,128)(2,1)S(1)}, u32[]{:S(2)}, u32[]{:S(2)}) %all-to-all-start.2) | async-done | bytes 1572896 | tf_op jit(solution)/shard_map/all_to_all | solution.py:88
  319.1 2.2 gather_fusion
  321.3 2.8 fusion.20
  324.1 1.6 fusion.19
  (50 shorter events, 5.8 us)
Async XLA Ops:
  6.5 111.2 %copy-start = (bf16[1,384,4096]{2,1,0:T(8,128)(2,1)S(1)}, bf16[1,384,4096]{2,1,0:T(8,128)(2,1)}, u32[]{:S(2)}) copy-start(bf16[1,384,4096]{2,1,0:T(8,128)(2,1)} %param.15) | copy-start | bytes 9437188
  6.5 6.0 %copy-start.12 = (f32[4096]{0:T(1024)S(1)}, f32[4096]{0:T(1024)}, u32[]{:S(2)}) copy-start(f32[4096]{0:T(1024)} %param.10) | copy-start | bytes 49156
  6.5 100.1 %all-gather.5.cloned.1.call-start = ((), (), s32[]{:S(2)}) async-start(), calls=%async_computation.7 | async-start | bytes 7864320 | tf_op jit(solution)/shard_map/all_gather | solution.py:18
  61.1 93.6 %all-gather.3.cloned.1.call-start = ((), (), s32[]{:S(2)}) async-start(), calls=%async_computation.6 | async-start | bytes 7864320 | tf_op jit(solution)/shard_map/all_gather | solution.py:18
  105.8 109.8 %reduce-scatter.5.cloned.1.call-start = ((), (), s32[]{:S(2)}) async-start(), calls=%async_computation.9 | async-start | bytes 7864320 | tf_op jit(solution)/shard_map/reduce_scatter | solution.py:59
  106.7 6.6 %copy-start.8 = (bf16[1,4096,384]{2,1,0:T(8,128)(2,1)S(1)}, bf16[1,4096,384]{2,1,0:T(8,128)(2,1)}, u32[]{:S(2)}) copy-start(bf16[1,4096,384]{2,1,0:T(8,128)(2,1)} %param.14) | copy-start | bytes 9437188
  106.7 6.6 %copy-start.13 = (bf16[1,32,24,4096]{3,2,0,1:T(8,128)(2,1)S(1)}, bf16[1,32,24,4096]{3,2,0,1:T(8,128)(2,1)}, u32[]{:S(2)}) copy-start(bf16[1,32,24,4096]{3,2,0,1:T(8,128)(2,1)} %all-gather.5.cloned.1.call-done) | copy-start | bytes 18874372
  113.3 3.4 %copy-start.4 = (f32[768,384]{1,0:T(8,128)}, f32[768,384]{1,0:T(8,128)S(1)}, u32[]{:S(2)}) copy-start(f32[768,384]{1,0:T(8,128)S(1)} %fusion.3) | copy-start | bytes 3538948
  116.7 1.0 copy-start.9
  123.1 153.5 %reduce-scatter.3.cloned.1.call-start = ((), (), s32[]{:S(2)}) async-start(), calls=%async_computation.8 | async-start | bytes 7864320 | tf_op jit(solution)/shard_map/reduce_scatter | solution.py:84
  154.7 6.7 %copy-start.5 = (f32[768,384]{1,0:T(8,128)S(1)}, f32[768,384]{1,0:T(8,128)}, u32[]{:S(2)}) copy-start(f32[768,384]{1,0:T(8,128)} %copy-done.4) | copy-start | bytes 3538948
  154.7 6.7 %copy-start.7 = (bf16[1,4096,384]{2,1,0:T(8,128)(2,1)S(1)}, bf16[1,4096,384]{2,1,0:T(8,128)(2,1)}, u32[]{:S(2)}) copy-start(bf16[1,4096,384]{2,1,0:T(8,128)(2,1)} %param.13) | copy-start | bytes 9437188
  154.7 6.7 %copy-start.10 = (f32[768,384]{1,0:T(8,128)S(1)}, f32[768,384]{1,0:T(8,128)}, u32[]{:S(2)}) copy-start(f32[768,384]{1,0:T(8,128)} %copy-done.9) | copy-start | bytes 3538948
  160.3 1.0 copy-start.6
  215.6 60.9 %all-to-all-start.3 = ((bf16[8,24,4096]{2,1,0:T(8,128)(2,1)}), bf16[8,24,4096]{2,1,0:T(8,128)(2,1)S(1)}, u32[]{:S(2)}, u32[]{:S(2)}) async-start(bf16[8,24,4096]{2,1,0:T(8,128)(2,1)} %bitcast.55), calls=%async_computation.5 | async-start | bytes 3145728 | tf_op jit(solution)/shard_map/all_to_all | solution.py:66
  276.5 42.5 %all-to-all-start.2 = ((bf16[8,24,4096]{2,1,0:T(8,128)(2,1)}), bf16[8,24,4096]{2,1,0:T(8,128)(2,1)S(1)}, u32[]{:S(2)}, u32[]{:S(2)}) async-start(bf16[8,24,4096]{2,1,0:T(8,128)(2,1)} %bitcast.56), calls=%async_computation.3 | async-start | bytes 3145728 | tf_op jit(solution)/shard_map/all_to_all | solution.py:88
  319.1 2.2 copy-start.2
  319.1 2.2 copy-start.11
  321.3 2.8 copy-start.3
  324.1 2.3 copy-start.1
Sparse Core Ops, SparseCore 0:
  61.2 45.4 all-gather.4
  108.2 46.3 all-gather.2
  157.2 58.3 reduce-scatter.4
  218.2 58.3 reduce-scatter.2
where the time goes:
time: 333 us
  waiting for transfers between devices  161 us (48%)
  blocking collectives  84.9 us (25%)
  matrix products  39.1 us (12%)
  other arithmetic  15.9 us (5%)
  between operations  13.3 us (4%)
  starting transfers between devices  11.3 us (3%)
  local copies, waits for them, and re-layouts  7.26 us (2%)
    all_to_all x2, blocking collectives, dispatch(): lax.all_to_all(shaped, 'ctx', split_axis=1, concat_axis=1, tiled=True)  84.9 us
    reduce_scatter x1, waiting for transfers between devices, per_device(): lax.psum_scatter((gate_part + up_part).astype(jnp.bfloat16), 'exp', scatt...  55.4 us
    reduce_scatter x1, waiting for transfers between devices, per_device(): lax.psum_scatter(jnp.dot(hidden, down_block, preferred_element_type=jnp.f...  40.5 us
    all_to_all x1, waiting for transfers between devices, per_device(): lax.all_to_all(grad_outgoing, 'ctx', split_axis=0, concat_axis=0, tiled=T...  32.9 us
    all_gather x2, waiting for transfers between devices, dispatch(): grouped = lax.all_gather(moved, 'exp', axis=1, tiled=True)  32.2 us
    dot_general x1, matrix products, per_device(): lax.dot_general(grad_pre_up, up_block, (((1,), (1,)), ((), ())), preferre...  10.1 us
    scatter x2, other arithmetic, place(): return empty.at[:, target, :].set(values)  8.26 us
  transfers between devices with their start and end apart: 6, of which 5 were waited for; matrix products, arithmetic and copies ran while one was open for 13% of the time, Pallas kernels for 0%

commit v1 on v0

v1 whole, which is shorter than its diff:
```python
import jax
import jax.numpy as jnp
from jax import lax
from jax.sharding import PartitionSpec as P

EPSILON = 1e-06
F32 = jnp.float32
BF16 = jnp.bfloat16


def pick(rows_of, total, values):
    hot = (rows_of[None, :] == jnp.arange(total, dtype=jnp.int32)[:, None]).astype(BF16)
    return jnp.dot(hot, values, preferred_element_type=F32).astype(BF16)


def expert_math(normed_rows, up_rows, gate_block, up_block, down_block):
    pre_gate = jnp.dot(normed_rows, gate_block, preferred_element_type=F32)
    pre_up = jnp.dot(normed_rows, up_block, preferred_element_type=F32)
    raw_grad = lax.dot_general(
        up_rows, down_block, (((1,), (1,)), ((), ())), preferred_element_type=F32
    )
    sig = jax.nn.sigmoid(pre_gate)
    act = pre_gate * sig
    slope = sig * (1.0 + pre_gate * (1.0 - sig))
    hidden = (act * pre_up).astype(BF16).astype(F32)
    dots = jnp.sum(hidden * raw_grad, axis=1)
    grad_gate = (raw_grad * pre_up * slope).astype(BF16)
    grad_up = (raw_grad * act).astype(BF16)
    back = lax.dot_general(
        grad_gate, gate_block, (((1,), (1,)), ((), ())), preferred_element_type=F32
    ) + lax.dot_general(grad_up, up_block, (((1,), (1,)), ((), ())), preferred_element_type=F32)
    return back, dots


def exchange_collective(slots_normed, slots_up, gate_block, up_block, down_block):
    experts, capacity, width = slots_normed.shape

    def dispatch(shaped):
        moved = lax.all_to_all(shaped, "ctx", split_axis=0, concat_axis=0, tiled=True)
        return lax.all_gather(
            moved.reshape(experts * capacity, width), "exp", axis=0, tiled=True
        )

    back, dots = expert_math(
        dispatch(slots_normed), dispatch(slots_up), gate_block, up_block, down_block
    )
    summed = lax.psum_scatter(back.astype(BF16), "exp", scatter_dimension=0, tiled=True)
    dot_sum = lax.psum_scatter(dots, "exp", scatter_dimension=0, tiled=True)
    returned = lax.all_to_all(
        summed.reshape(experts, capacity, width), "ctx", split_axis=0, concat_axis=0, tiled=True
    )
    dot_back = lax.all_to_all(
        dot_sum.reshape(experts, capacity), "ctx", split_axis=0, concat_axis=0, tiled=True
    )
    return returned.reshape(experts * capacity, width), dot_back.reshape(experts * capacity)


def per_device(hidden_states, upstream, norm_gain, router, expert_ids, w_gate, w_up, w_down):
    tok_rows, model_width = hidden_states.shape
    experts = router.shape[1]
    capacity = 3 * tok_rows // (2 * experts)
    slot_total = experts * capacity
    labels = jnp.arange(experts, dtype=jnp.int32)
    chosen = (expert_ids[:, :, None] == labels).astype(F32)
    primary = chosen[:, 0, :]
    member = jnp.sum(chosen, axis=1)
    lower = (
        jnp.arange(tok_rows)[:, None] > jnp.arange(tok_rows)[None, :]
    ).astype(BF16)
    before = jnp.dot(lower, primary.astype(BF16), preferred_element_type=F32)
    slot_index = jnp.sum(before * primary, axis=1).astype(jnp.int32)
    target = expert_ids[:, 0] * capacity + slot_index

    widened = hidden_states.astype(F32)
    inverse = lax.rsqrt(jnp.mean(widened * widened, axis=1, keepdims=True) + EPSILON)
    normed = (widened * inverse * norm_gain).astype(BF16)

    slots_up = pick(target, slot_total, upstream).reshape(experts, capacity, model_width)
    slots_normed = pick(target, slot_total, normed).reshape(experts, capacity, model_width)
    returned, dots = exchange_collective(slots_normed, slots_up, w_gate[0], w_up[0], w_down[0])

    logits = jnp.dot(normed, router, preferred_element_type=F32)
    probability = jax.nn.softmax(logits, axis=1)
    top_prob = jnp.sum(probability * primary, axis=1)
    route_mass = jnp.sum(probability * member, axis=1)
    gate_value = top_prob / route_mass

    own = target[:, None] == jnp.arange(slot_total, dtype=jnp.int32)[None, :]
    raw_back = jnp.dot(own.astype(BF16), returned, preferred_element_type=F32)
    gate_grad = jnp.sum(jnp.where(own, dots[None, :], 0.0), axis=1)
    expert_grad = gate_value[:, None] * raw_back
    prob_grad = gate_grad[:, None] * (
        primary / route_mass[:, None] - (top_prob / (route_mass * route_mass))[:, None] * member
    )
    logit_grad = probability * (prob_grad - jnp.sum(probability * prob_grad, axis=1, keepdims=True))
    normed_grad = expert_grad + jnp.dot(
        logit_grad, router.astype(F32).T, precision=lax.Precision.HIGHEST
    )
    scaled = normed_grad * norm_gain
    grad_input = (
        inverse * scaled
        - widened * inverse**3 * jnp.sum(scaled * widened, axis=1, keepdims=True) / model_width
    )
    return grad_input.astype(BF16)


def solution(mesh):
    placed = (
        P(("ctx", "exp"), None),
        P(("ctx", "exp"), None),
        P(),
        P(),
        P(("ctx", "exp"), None),
        P("ctx", None, "exp"),
        P("ctx", None, "exp"),
        P("ctx", "exp", None),
    )
    return jax.shard_map(
        per_device, mesh=mesh, in_specs=placed, out_specs=P(("ctx", "exp"), None), check_vma=False
    )
```

time: 333 us -> 285 us (0.86)
  waiting for transfers between devices: 161 us -> 114 us
  blocking collectives: 84.9 us -> 102 us
  other arithmetic: 15.9 us -> 5.53 us
  starting transfers between devices: 11.3 us -> 5.74 us
  local copies, waits for them, and re-layouts: 7.26 us -> 1.99 us
    reduce_scatter x2 -> x1, waiting for transfers between devices: 96 us -> 38.7 us  [exchange_collective(): lax.psum_scatter(back.astype(BF16), 'exp', scatter_dimension=0, tiled=True)]
    all_to_all x2 -> x3, blocking collectives: 84.9 us -> 96.3 us  [the longest x2 84.3 us: dispatch(): lax.all_to_all(shaped, 'ctx', split_axis=0, concat_axis=0, tiled=True)]
    all_gather x2, waiting for transfers between devices: 32.2 us -> 41.2 us  [dispatch(): lax.all_gather(moved.reshape(experts * capacity, width), 'exp', axis=0, t...]
    scatter x2 -> x0, other arithmetic: 8.26 us -> none  [place(): return empty.at[:, target, :].set(values)]
    unnamed x0 -> x1, blocking collectives: none -> 5.92 us
    all_to_all x2 -> x1, starting transfers between devices: 11 us -> 5.65 us  [exchange_collective(): lax.all_to_all(summed.reshape(experts, capacity, width), 'ctx', split_axi...]
    gather x2 -> x0, local copies, waits for them, and re-layouts: 4.33 us -> none  [the longest x1 2.16 us: per_device(): expert_out = returned[target].astype(jnp.float32)]
    dot_general x8 -> x11, matrix products: 39.1 us -> 41.4 us  [the longest x1 8.24 us: expert_math(): lax.dot_general(grad_up, up_block, (((1,), (1,)), ((), ())), preferred_el...]
  transfers between devices with their start and end apart: 6 -> 4, of which waited for: 5 -> 4; matrix products, arithmetic and copies ran while one was open for 13% -> 6% of each run, Pallas kernels for 0% -> 0%
where the time goes in v1:
time: 285 us
  waiting for transfers between devices  114 us (40%)
  blocking collectives  102 us (36%)
  matrix products  41.4 us (15%)
  between operations  13.9 us (5%)
  starting transfers between devices  5.74 us (2%)
  other arithmetic  5.53 us (2%)
    all_to_all x2, blocking collectives, dispatch(): lax.all_to_all(shaped, 'ctx', split_axis=0, concat_axis=0, tiled=True)  84.3 us
    all_gather x2, waiting for transfers between devices, dispatch(): lax.all_gather(moved.reshape(experts * capacity, width), 'exp', axis=0, t...  41.2 us
    reduce_scatter x1, waiting for transfers between devices, exchange_collective(): lax.psum_scatter(back.astype(BF16), 'exp', scatter_dimension=0, tiled=True)  38.7 us
    all_to_all x1, waiting for transfers between devices, exchange_collective(): lax.all_to_all(summed.reshape(experts, capacity, width), 'ctx', split_axi...  33.9 us
    all_to_all x1, blocking collectives, exchange_collective(): lax.all_to_all(dot_sum.reshape(experts, capacity), 'ctx', split_axis=0, c...  11.9 us
    dot_general x1, matrix products, expert_math(): lax.dot_general(grad_up, up_block, (((1,), (1,)), ((), ())), preferred_el...  8.24 us
    dot_general x1, matrix products, expert_math(): lax.dot_general(up_rows, down_block, (((1,), (1,)), ((), ())), preferred_...  7.2 us
    dot_general x1, matrix products, expert_math(): lax.dot_general(grad_gate, gate_block, (((1,), (1,)), ((), ())), preferre...  6.78 us
  transfers between devices with their start and end apart: 4, of which 4 were waited for; matrix products, arithmetic and copies ran while one was open for 6% of the time, Pallas kernels for 0%

profile of v1, /device:TPU:0, one launch (start us, length us, event | category | flops | bytes accessed | tf_op | source)
XLA Modules:
  0.0 284.5 jit_solution(2468157906143429721)
XLA Ops:
  6.5 0.8 fusion.28
  7.5 0.7 bitcast_add_fusion
  8.2 1.5 fusion.10
  9.8 1.9 convolution_convert_fusion
  11.7 44.2 %all_to_all.24 = bf16[8,24,4096]{2,1,0:T(8,128)(2,1)} all-to-all(bf16[8,24,4096]{2,1,0:T(8,128)(2,1)S(1)} %bitcast.58), channel_id=1, replica_groups=mesh['ctx'=8,'exp'=4] {'ctx'}, dimensions={0} | all-to-all | bytes 3145728 | tf_op jit(solution)/shard_map/all_to_all | solution.py:39
  55.9 1.8 convolution_convert_fusion.1
  57.7 40.2 %all_to_all.25 = bf16[8,24,4096]{2,1,0:T(8,128)(2,1)} all-to-all(bf16[8,24,4096]{2,1,0:T(8,128)(2,1)S(1)} %bitcast.57), channel_id=1, replica_groups=mesh['ctx'=8,'exp'=4] {'ctx'}, dimensions={0} | all-to-all | bytes 3145728 | tf_op jit(solution)/shard_map/all_to_all | solution.py:39
  97.9 3.5 %all-gather.5.cloned.1.call-done = bf16[768,4096]{1,0:T(8,128)(2,1)} async-done(((bf16[192,4096]{1,0:T(8,128)(2,1)}), bf16[768,4096]{1,0:T(8,128)(2,1)}) %all-gather.5.cloned.1.call-update) | async-done | bytes 6291472 | tf_op jit(solution)/shard_map/all_gather | solution.py:40
  101.4 6.6 %fusion.3 = f32[768,384]{0,1:T(8,128)} fusion(bf16[768,4096]{1,0:T(8,128)(2,1)} %all-gather.5.cloned.1.call-done, bf16[1,4096,384]{2,1,0:T(8,128)(2,1)S(1)} %copy-done), kind=kOutput, calls=%fused_computation.12 | convolution fusion | flops 2415919104 | bytes 10616832 | tf_op jit(solution)/shard_map/dot_general | solution.py:17
  108.0 3.7 %fusion.6 = f32[768,384]{0,1:T(8,128)} fusion(bf16[768,4096]{1,0:T(8,128)(2,1)S(1)} %copy-done.9, bf16[1,4096,384]{2,1,0:T(8,128)(2,1)S(1)} %copy-done.3), kind=kOutput, calls=%fused_computation.15 | convolution fusion | flops 2415919104 | bytes 10616832 | tf_op jit(solution)/shard_map/dot_general | solution.py:18
  111.7 37.7 %all-gather.3.cloned.1.call-done = bf16[768,4096]{1,0:T(8,128)(2,1)} async-done(((bf16[192,4096]{1,0:T(8,128)(2,1)}), bf16[768,4096]{1,0:T(8,128)(2,1)}) %all-gather.3.cloned.1.call-update) | async-done | bytes 6291472 | tf_op jit(solution)/shard_map/all_gather | solution.py:40
  149.4 7.2 %multiply_reduce_fusion = (f32[768]{0:T(1024)S(1)}, f32[768,384]{0,1:T(8,128)S(1)}) fusion(f32[768,384]{0,1:T(8,128)} %fusion.6, f32[768,384]{0,1:T(8,128)} %fusion.3, bf16[768,4096]{1,0:T(8,128)(2,1)} %all-gather.3.cloned.1.call-done, bf16[1,384,4096]{2,1,0:T(8,128)(2,1)} %param.15), kind=kOutput, calls=%fused_computation.27 | convolution fusion | flops 2418572544 | bytes 12979200 | tf_op jit(solution)/shard_map/dot_general | solution.py:19
  156.6 6.8 %fusion.1 = f32[768,4096]{1,0:T(8,128)} fusion(bf16[1,4096,384]{2,1,0:T(8,128)(2,1)S(1)} %copy-done, f32[768,384]{0,1:T(8,128)S(1)} %copy-done.2, f32[768,384]{0,1:T(8,128)S(1)} %get-tuple-element.14, f32[768,384]{0,1:T(8,128)S(1)} %copy-done.5), kind=kOutput, calls=%fused_computation.10 | convolution fusion | flops 2418868224 | bytes 19267584 | tf_op jit(solution)/shard_map/dot_general | solution.py:29
  163.4 8.2 %add_convert_fusion = bf16[768,4096]{1,0:T(8,128)(2,1)} fusion(f32[768,4096]{1,0:T(8,128)} %fusion.1, bf16[1,4096,384]{2,1,0:T(8,128)(2,1)S(1)} %copy-done.4, f32[768,384]{0,1:T(8,128)S(1)} %get-tuple-element.14, f32[768,384]{0,1:T(8,128)S(1)} %copy-done.2), kind=kOutput, calls=%fused_computation | convolution fusion | flops 2423980032 | bytes 24379392 | tf_op jit(solution)/shard_map/dot_general | solution.py:31
  173.6 5.9 %all-reduce = f32[768]{0:T(1024)S(1)} all-reduce(f32[768]{0:T(1024)S(1)} %get-tuple-element.13), channel_id=3, replica_groups=mesh['ctx'=8,'exp'=4] {'exp'}, use_global_device_ids=true, to_apply=%region_9.0.clone | all-reduce | flops 768 | bytes 6144
  179.6 11.9 %all_to_all.26 = f32[8,1,24]{2,1,0:T(1,128)S(1)} all-to-all(f32[8,1,24]{2,1,0:T(1,128)S(1)} %all_to_all.18), channel_id=1, replica_groups=mesh['ctx'=8,'exp'=4] {'ctx'}, dimensions={0} | all-to-all | bytes 1536 | tf_op jit(solution)/shard_map/all_to_all | solution.py:52
  191.6 38.7 %reduce-scatter.2.cloned.1.call-done = bf16[192,4096]{1,0:T(8,128)(2,1)} async-done(((bf16[768,4096]{1,0:T(8,128)(2,1)}), bf16[192,4096]{1,0:T(8,128)(2,1)}) %reduce-scatter.2.cloned.1.call-update) | async-done | bytes 1572880 | tf_op jit(solution)/shard_map/reduce_scatter | solution.py:47
  230.2 5.7 %all-to-all-start.2 = ((bf16[8,24,4096]{2,1,0:T(8,128)(2,1)}), bf16[8,24,4096]{2,1,0:T(8,128)(2,1)}, u32[]{:S(2)}, u32[]{:S(2)}) async-start(bf16[8,24,4096]{2,1,0:T(8,128)(2,1)} %bitcast.59), calls=%async_computation.3 | async-start | bytes 3145728 | tf_op jit(solution)/shard_map/all_to_all | solution.py:49
  235.9 1.7 fusion.41
  238.2 0.7 reduce.3
  239.1 33.9 %all-to-all-done.2 = bf16[8,24,4096]{2,1,0:T(8,128)(2,1)} async-done(((bf16[8,24,4096]{2,1,0:T(8,128)(2,1)}), bf16[8,24,4096]{2,1,0:T(8,128)(2,1)}, u32[]{:S(2)}, u32[]{:S(2)}) %all-to-all-start.2) | async-done | bytes 1572896 | tf_op jit(solution)/shard_map/all_to_all | solution.py:49
  273.0 2.0 convolution_multiply_fusion
  275.0 1.4 fusion.17
  276.4 1.6 fusion.16
  (42 shorter events, 2.5 us)
Async XLA Ops:
  6.5 94.9 %copy-start = (bf16[1,4096,384]{2,1,0:T(8,128)(2,1)S(1)}, bf16[1,4096,384]{2,1,0:T(8,128)(2,1)}, u32[]{:S(2)}) copy-start(bf16[1,4096,384]{2,1,0:T(8,128)(2,1)} %param.13) | copy-start | bytes 9437188
  6.5 94.9 %all-gather.5.cloned.1.call-start = ((), (), s32[]{:S(2)}) async-start(), calls=%async_computation.6 | async-start | bytes 7864320 | tf_op jit(solution)/shard_map/all_gather | solution.py:40
  55.8 93.6 %all-gather.3.cloned.1.call-start = ((), (), s32[]{:S(2)}) async-start(), calls=%async_computation.5 | async-start | bytes 7864320 | tf_op jit(solution)/shard_map/all_gather | solution.py:40
  97.9 132.3 %reduce-scatter.2.cloned.1.call-start = ((), (), s32[]{:S(2)}) async-start(), calls=%async_computation.7 | async-start | bytes 7864320 | tf_op jit(solution)/shard_map/reduce_scatter | solution.py:47
  101.4 6.6 %copy-start.3 = (bf16[1,4096,384]{2,1,0:T(8,128)(2,1)S(1)}, bf16[1,4096,384]{2,1,0:T(8,128)(2,1)}, u32[]{:S(2)}) copy-start(bf16[1,4096,384]{2,1,0:T(8,128)(2,1)} %param.14) | copy-start | bytes 9437188
  101.4 6.6 %copy-start.9 = (bf16[768,4096]{1,0:T(8,128)(2,1)S(1)}, bf16[768,4096]{1,0:T(8,128)(2,1)}, u32[]{:S(2)}) copy-start(bf16[768,4096]{1,0:T(8,128)(2,1)} %all-gather.5.cloned.1.call-done) | copy-start | bytes 18874372
  149.4 7.2 %copy-start.2 = (f32[768,384]{0,1:T(8,128)S(1)}, f32[768,384]{0,1:T(8,128)}, u32[]{:S(2)}) copy-start(f32[768,384]{0,1:T(8,128)} %fusion.3) | copy-start | bytes 3538948
  149.4 7.2 %copy-start.5 = (f32[768,384]{0,1:T(8,128)S(1)}, f32[768,384]{0,1:T(8,128)}, u32[]{:S(2)}) copy-start(f32[768,384]{0,1:T(8,128)} %fusion.6) | copy-start | bytes 3538948
  156.6 6.8 %copy-start.4 = (bf16[1,4096,384]{2,1,0:T(8,128)(2,1)S(1)}, bf16[1,4096,384]{2,1,0:T(8,128)(2,1)}, u32[]{:S(2)}) copy-start(bf16[1,4096,384]{2,1,0:T(8,128)(2,1)} %param.14) | copy-start | bytes 9437188
  171.7 0.7 copy-start.10
  171.7 64.2 %copy-start.6 = (bf16[4096,8]{0,1:T(8,128)(2,1)S(1)}, bf16[4096,8]{0,1:T(8,128)(2,1)}, u32[]{:S(2)}) copy-start(bf16[4096,8]{0,1:T(8,128)(2,1)} %param.11) | copy-start | bytes 196612
  171.7 64.2 %copy-start.7 = (f32[4096]{0:T(1024)S(1)}, f32[4096]{0:T(1024)}, u32[]{:S(2)}) copy-start(f32[4096]{0:T(1024)} %param.10) | copy-start | bytes 49156
  230.2 7.4 %copy-start.8 = (s32[128,8]{0,1:T(8,128)S(1)}, s32[128,8]{0,1:T(8,128)}, u32[]{:S(2)}) copy-start(s32[128,8]{0,1:T(8,128)} %param.12) | copy-start | bytes 12292
  230.2 42.8 %all-to-all-start.2 = ((bf16[8,24,4096]{2,1,0:T(8,128)(2,1)}), bf16[8,24,4096]{2,1,0:T(8,128)(2,1)}, u32[]{:S(2)}, u32[]{:S(2)}) async-start(bf16[8,24,4096]{2,1,0:T(8,128)(2,1)} %bitcast.59), calls=%async_computation.3 | async-start | bytes 3145728 | tf_op jit(solution)/shard_map/all_to_all | solution.py:49
  273.0 2.0 copy-start.1
Sparse Core Ops, SparseCore 0:
  56.0 45.4 all-gather.4
  103.0 46.3 all-gather.2
  171.8 58.3 reduce-scatter.1

commit v2 on v1

--- a/solution.py
+++ b/solution.py
@@ -1,11 +1,18 @@
+import functools
+
 import jax
 import jax.numpy as jnp
 from jax import lax
+from jax.experimental import pallas as pl
+from jax.experimental.pallas import tpu as pltpu
 from jax.sharding import PartitionSpec as P
 
 EPSILON = 1e-06
 F32 = jnp.float32
 BF16 = jnp.bfloat16
+LANES = 128
+DEEP = 1024
+WIDE = 512
 
 
 def pick(rows_of, total, values):
@@ -53,6 +60,275 @@
         dot_sum.reshape(experts, capacity), "ctx", split_axis=0, concat_axis=0, tiled=True
     )
     return returned.reshape(experts * capacity, width), dot_back.reshape(experts * capacity)
+
+
+def exclusive_or(left, right, count):
+    total, bit = 0, 1
+    while bit < count:
+        total = total + bit * lax.rem(lax.div(left, bit) + lax.div(right, bit), 2)
+        bit *= 2
+    return total
+
+
+def ordered(step, count):
+    return lax.rem(step, 2) * (count // 2) + lax.div(step, 2)
+
+
+def carry(total, width, capacity):
+    dots = total[:capacity, width:] + total[capacity:, width:]
+    high = dots.astype(BF16).astype(F32)
+    return total[:, :width].astype(BF16), jnp.concatenate([high, dots - high], axis=0).astype(BF16)
+
+
+def exchange_body(
+    count, capacity, send_ref, gate_hbm, up_hbm, down_hbm, out_ref,
+    both, down, rows, part, mate_in, mid, cross_in, done, acc_both, acc_down, grads,
+    weight_sem, local_sem, send_sem, recv_sem,
+):
+    width = send_ref.shape[2]
+    half = width // 2
+    units = down.shape[0]
+    tall = -(-capacity // 16) * 16
+    skip = tall - capacity
+    ctx = lax.axis_index("ctx")
+    exp = lax.axis_index("exp")
+    row, core = lax.div(exp, 2), lax.rem(exp, 2)
+    mate = row * 2 + (1 - core)
+    cross = (1 - row) * 2 + core
+
+    def remote(src, dst, kind, k, device):
+        return pltpu.make_async_remote_copy(
+            src_ref=src, dst_ref=dst, send_sem=send_sem.at[kind, k], recv_sem=recv_sem.at[kind, k],
+            device_id=device, device_id_type=pl.DeviceIdType.MESH,
+        )
+
+    def partner(k):
+        return exclusive_or(ctx, k, count)
+
+    def direct(k):
+        return remote(send_ref.at[partner(k)], rows.at[k, exp], 0, k, (partner(k), exp))
+
+    def to_mate(k):
+        return remote(rows.at[k, exp], rows.at[k, exp], 1, k, (ctx, mate))
+
+    def to_cross(k):
+        return remote(rows.at[k, exp], rows.at[k, exp], 2, k, (ctx, cross))
+
+    def relay(k):
+        return remote(rows.at[k, cross], rows.at[k, cross], 3, k, (ctx, mate))
+
+    def part_to_mate(k):
+        return remote(part.at[k, 1 - core], mate_in.at[k], 4, k, (ctx, mate))
+
+    def sum_to_cross(k):
+        return remote(mid.at[k], cross_in.at[k], 5, k, (ctx, cross))
+
+    def give_back(k):
+        return remote(done.at[k], out_ref.at[ctx], 6, k, (partner(k), exp))
+
+    def self_in():
+        return pltpu.make_async_copy(send_ref.at[ctx], rows.at[0, exp], local_sem.at[0])
+
+    def self_out():
+        return pltpu.make_async_copy(done.at[0], out_ref.at[ctx], local_sem.at[1])
+
+    weights = [
+        pltpu.make_async_copy(gate_hbm.at[0], both.at[:, pl.ds(0, units)], weight_sem.at[0]),
+        pltpu.make_async_copy(up_hbm.at[0], both.at[:, pl.ds(units, units)], weight_sem.at[1]),
+        pltpu.make_async_copy(down_hbm.at[0], down, weight_sem.at[2]),
+    ]
+    for copy in weights:
+        copy.start()
+    self_in().start()
+
+    barrier = pltpu.get_barrier_semaphore()
+
+    @pl.loop(1, count)
+    def _(k):
+        pl.semaphore_signal(
+            barrier, inc=1, device_id=(partner(k), exp), device_id_type=pl.DeviceIdType.MESH
+        )
+
+    for other in (mate, cross):
+        pl.semaphore_signal(
+            barrier, inc=1, device_id=(ctx, other), device_id_type=pl.DeviceIdType.MESH
+        )
+    pl.semaphore_wait(barrier, count + 1)
+
+    @pl.loop(1, count)
+    def _(step):
+        direct(ordered(step, count)).start()
+
+    def compute(k):
+        acc_both[...] = jnp.zeros_like(acc_both)
+        acc_down[...] = jnp.zeros_like(acc_down)
+        deep = DEEP
+
+        @pl.loop(0, width // deep)
+        def _(j):
+            columns = pl.ds(pl.multiple_of(j * deep, deep), deep)
+            acc_both[...] += jnp.dot(
+                rows[k, :, pl.ds(0, tall), columns].reshape(4 * tall, deep),
+                both[columns, :],
+                preferred_element_type=F32,
+            )
+            acc_down[...] += lax.dot_general(
+                rows[k, :, pl.ds(2 * capacity - tall, tall), columns].reshape(4 * tall, deep),
+                down[:, columns],
+                (((1,), (1,)), ((), ())),
+                preferred_element_type=F32,
+            )
+
+        pre_gate = acc_both[:, :units].reshape(4, tall, units)[:, :capacity]
+        pre_up = acc_both[:, units:].reshape(4, tall, units)[:, :capacity]
+        raw_grad = acc_down[...].reshape(4, tall, units)[:, skip:]
+        sig = jax.nn.sigmoid(pre_gate)
+        act = pre_gate * sig
+        slope = sig * (1.0 + pre_gate * (1.0 - sig))
+        hidden = (act * pre_up).astype(BF16).astype(F32)
+        dots = jnp.sum(hidden * raw_grad, axis=2, keepdims=True)
+        high = dots.astype(BF16).astype(F32)
+        tail = jnp.concatenate([high, dots - high], axis=1)
+        tail = jnp.broadcast_to(tail, (4, 2 * capacity, LANES)).astype(BF16)
+        for one in range(4):
+            part[k, one % 2, one // 2, :, pl.ds(half, LANES)] = tail[one]
+        grads[:, :units] = (raw_grad * pre_up * slope).reshape(4 * capacity, units).astype(BF16)
+        grads[:, units:] = (raw_grad * act).reshape(4 * capacity, units).astype(BF16)
+
+        @pl.loop(0, half // WIDE)
+        def _(j):
+            sides = []
+            for side in range(2):
+                start = pl.multiple_of(side * half + j * WIDE, WIDE)
+                product = lax.dot_general(
+                    grads[...],
+                    both[pl.ds(start, WIDE), :],
+                    (((1,), (1,)), ((), ())),
+                    preferred_element_type=F32,
+                )
+                sides.append(product.reshape(4, capacity, WIDE))
+            value = jnp.concatenate(sides, axis=1).astype(BF16)
+            columns = pl.ds(pl.multiple_of(j * WIDE, WIDE), WIDE)
+            for one in range(4):
+                part[k, one % 2, one // 2, :, columns] = value[one]
+
+    def stage(step, lag):
+        return pl.when(jnp.logical_and(step >= lag, step < count + lag))
+
+    @pl.loop(0, count + 4)
+    def _(step):
+        @pl.when(step == 0)
+        def _():
+            self_in().wait()
+
+        @pl.when(jnp.logical_and(step >= 1, step < count))
+        def _():
+            direct(ordered(step, count)).wait_recv()
+
+        @stage(step, 0)
+        def _():
+            k = ordered(step, count)
+            to_cross(k).start()
+            to_mate(k).start()
+
+        @stage(step, 1)
+        def _():
+            k = ordered(step - 1, count)
+            to_cross(k).wait_recv()
+            relay(k).start()
+
+        @pl.when(step == 2)
+        def _():
+            for copy in weights:
+                copy.wait()
+
+        @stage(step, 2)
+        def _():
+            k = ordered(step - 2, count)
+            to_mate(k).wait_recv()
+            relay(k).wait_recv()
+            compute(k)
+            part_to_mate(k).start()
+
+        @stage(step, 3)
+        def _():
+            k = ordered(step - 3, count)
+            part_to_mate(k).wait_recv()
+            total = part[k, core, 1 - row].astype(F32) + mate_in[k, 1 - row].astype(F32)
+            body, tail = carry(total, half, capacity)
+            mid[k, :, pl.ds(0, half)] = body
+            mid[k, :, pl.ds(half, LANES)] = tail
+            sum_to_cross(k).start()
+
+        def finish(k):
+            sum_to_cross(k).wait_recv()
+            total = part[k, core, row].astype(F32) + mate_in[k, row].astype(F32)
+            total = total + cross_in[k].astype(F32)
+            body, tail = carry(total, half, capacity)
+            done[k, :, pl.ds(0, half)] = body
+            done[k, :, pl.ds(half, LANES)] = tail
+
+        @stage(step, 4)
+        def _():
+            finish(ordered(step - 4, count))
+
+        @pl.when(step == 4)
+        def _():
+            self_out().start()
+
+        @pl.when(jnp.logical_and(step > 4, step < count + 4))
+        def _():
+            give_back(ordered(step - 4, count)).start()
+
+    self_out().wait()
+
+    @pl.loop(1, count)
+    def _(k):
+        give_back(k).wait()
+        direct(k).wait_send()
+
+    @pl.loop(0, count)
+    def _(k):
+        to_mate(k).wait_send()
+        to_cross(k).wait_send()
+        relay(k).wait_send()
+        part_to_mate(k).wait_send()
+        sum_to_cross(k).wait_send()
+
+
+def exchange_kernel(slots, capacity, w_gate, w_up, w_down):
+    count, tall, width = slots.shape
+    units = w_down.shape[1]
+    wide = width // 2 + LANES
+    rows_up = 4 * (-(-capacity // 16) * 16)
+    vmem = pl.BlockSpec(memory_space=pltpu.VMEM)
+    hbm = pl.BlockSpec(memory_space=pl.ANY)
+    return pl.pallas_call(
+        functools.partial(exchange_body, count, capacity),
+        out_shape=jax.ShapeDtypeStruct((count, tall, wide), BF16),
+        in_specs=[vmem, hbm, hbm, hbm],
+        out_specs=vmem,
+        scratch_shapes=[
+            pltpu.VMEM((width, 2 * units), BF16),
+            pltpu.VMEM((units, width), BF16),
+            pltpu.VMEM((count, 4, tall, width), BF16),
+            pltpu.VMEM((count, 2, 2, tall, wide), BF16),
+            pltpu.VMEM((count, 2, tall, wide), BF16),
+            pltpu.VMEM((count, tall, wide), BF16),
+            pltpu.VMEM((count, tall, wide), BF16),
+            pltpu.VMEM((count, tall, wide), BF16),
+            pltpu.VMEM((rows_up, 2 * units), F32),
+            pltpu.VMEM((rows_up, units), F32),
+            pltpu.VMEM((4 * capacity, 2 * units), BF16),
+            pltpu.SemaphoreType.DMA((3,)),
+            pltpu.SemaphoreType.DMA((2,)),
+            pltpu.SemaphoreType.DMA((7, count)),
+            pltpu.SemaphoreType.DMA((7, count)),
+        ],
+        compiler_params=pltpu.CompilerParams(
+            collective_id=0, has_side_effects=True, vmem_limit_bytes=56 * 2**20
+        ),
+    )(slots, w_gate, w_up, w_down)
 
 
 def per_device(hidden_states, upstream, norm_gain, router, expert_ids, w_gate, w_up, w_down):
@@ -75,9 +351,29 @@
     inverse = lax.rsqrt(jnp.mean(widened * widened, axis=1, keepdims=True) + EPSILON)
     normed = (widened * inverse * norm_gain).astype(BF16)
 
-    slots_up = pick(target, slot_total, upstream).reshape(experts, capacity, model_width)
-    slots_normed = pick(target, slot_total, normed).reshape(experts, capacity, model_width)
-    returned, dots = exchange_collective(slots_normed, slots_up, w_gate[0], w_up[0], w_down[0])
+    use_kernel = capacity % 8 == 0 and lax.axis_size("exp") == 4 and experts == 8
+    if use_kernel:
+        place = expert_ids[:, 0] * (2 * capacity) + slot_index
+        slots = pick(
+            jnp.concatenate([place, place + capacity]),
+            2 * slot_total,
+            jnp.concatenate([normed, upstream], axis=0),
+        )
+        packed = exchange_kernel(
+            slots.reshape(experts, 2 * capacity, model_width), capacity, w_gate, w_up, w_down
+        )
+        half = model_width // 2
+        low, high = packed[:, :capacity], packed[:, capacity:]
+        returned = jnp.concatenate([low[:, :, :half], high[:, :, :half]], axis=2)
+        returned = returned.reshape(slot_total, model_width)
+        dots = low[:, :, half].astype(F32) + high[:, :, half].astype(F32)
+        dots = dots.reshape(slot_total)
+    else:
+        slots_up = pick(target, slot_total, upstream).reshape(experts, capacity, model_width)
+        slots_normed = pick(target, slot_total, normed).reshape(experts, capacity, model_width)
+        returned, dots = exchange_collective(
+            slots_normed, slots_up, w_gate[0], w_up[0], w_down[0]
+        )
 
     logits = jnp.dot(normed, router, preferred_element_type=F32)
     probability = jax.nn.softmax(logits, axis=1)

time: 285 us -> 162 us (0.57)
  Pallas kernels: 0 us -> 145 us
  waiting for transfers between devices: 114 us -> 0 us
  blocking collectives: 102 us -> 0 us
  matrix products: 41.4 us -> 5.08 us
  between operations: 13.9 us -> 0.1 us
  starting transfers between devices: 5.74 us -> 0 us
  other arithmetic: 5.53 us -> 8.81 us
    pallas_call x0 -> x1, Pallas kernels: none -> 145 us  [exchange_kernel(): pl.pallas_call(functools.partial(exchange_body, count, capacity), out_sha...]
    all_to_all x3 -> x0, blocking collectives: 96.3 us -> none  [the longest x2 84.3 us: dispatch(): lax.all_to_all(shaped, 'ctx', split_axis=0, concat_axis=0, tiled=True)]
    all_gather x2 -> x0, waiting for transfers between devices: 41.2 us -> none  [dispatch(): lax.all_gather(moved.reshape(experts * capacity, width), 'exp', axis=0, t...]
    reduce_scatter x1 -> x0, waiting for transfers between devices: 38.7 us -> none  [exchange_collective(): lax.psum_scatter(back.astype(BF16), 'exp', scatter_dimension=0, tiled=True)]
    all_to_all x1 -> x0, waiting for transfers between devices: 33.9 us -> none  [exchange_collective(): lax.all_to_all(summed.reshape(experts, capacity, width), 'ctx', split_axi...]
    dot_general x5 -> x0, matrix products: 32.5 us -> none  [the longest x1 8.24 us: expert_math(): lax.dot_general(grad_up, up_block, (((1,), (1,)), ((), ())), preferred_el...]
    unnamed x1 -> x0, blocking collectives: 5.92 us -> none
    all_to_all x1 -> x0, starting transfers between devices: 5.65 us -> none  [exchange_collective(): lax.all_to_all(summed.reshape(experts, capacity, width), 'ctx', split_axi...]
  transfers between devices with their start and end apart: 4 -> 0, of which waited for: 4 -> 0; matrix products, arithmetic and copies ran while one was open for 6% -> 0% of each run, Pallas kernels for 0% -> 0%
where the time goes in v2:
time: 162 us
  Pallas kernels  145 us (90%)
  other arithmetic  8.81 us (5%)
  matrix products  5.08 us (3%)
  local copies, waits for them, and re-layouts  2.26 us (1%)
    pallas_call x1, Pallas kernels, exchange_kernel(): pl.pallas_call(functools.partial(exchange_body, count, capacity), out_sha...  145 us

profile of v2, /device:TPU:0, one launch (start us, length us, event | category | flops | bytes accessed | tf_op | source)
XLA Modules:
  0.0 161.6 jit_solution(2730068685332080634)
XLA Ops:
  0.0 0.0 copy-start
  0.0 1.6 fusion.1
  1.6 0.7 fusion.16
  2.3 0.7 fusion.15
  3.0 0.1 fusion.12
  3.2 0.7 fusion.24
  3.9 0.7 broadcast_add_fusion
  4.6 1.6 fusion.3
  6.2 0.0 copy-done
  6.2 0.4 fusion.28
  6.6 0.0 copy-done.3
  6.7 2.7 %convolution_convert_fusion = bf16[384,4096]{1,0:T(8,128)(2,1)} fusion(bf16[128,4096]{1,0:T(8,128)(2,1)S(1)} %copy-done.3, bf16[128,4096]{1,0:T(8,128)(2,1)S(1)} %fusion.3, s32[256]{0:T(256)S(1)} %pad_add_fusion), kind=kOutput, calls=%fused_computation | convolution fusion | flops 811171840 | bytes 5243904 | tf_op jit(solution)/shard_map/dot_general | solution.py:20
  9.3 145.3 %shard_map.82 = bf16[8,48,2176]{2,1,0:T(8,128)(2,1)} custom-call(bf16[8,48,4096]{2,1,0:T(8,128)(2,1)} %bitcast.34, bf16[1,4096,384]{2,1,0:T(8,128)(2,1)} %gate_hbm.1, bf16[1,4096,384]{2,1,0:T(8,128)(2,1)} %up_hbm.1, bf16[1,384,4096]{2,1,0:T(8,128)(2,1)} %down_hbm.1), custom_call_target="tpu_custom_call" | custom-call | tf_op jit(solution)/shard_map/pallas_call | solution.py:306
  154.7 0.9 add_reduce_fusion
  155.6 1.5 fusion.27
  157.1 0.1 add.43
  157.2 0.1 select_reduce_fusion
  157.3 0.1 pad_maximum_fusion
  157.4 0.0 copy-start.1
  157.4 0.0 copy-start.2
  157.4 0.5 convolution_multiply_fusion
  157.9 0.7 copy-done.1
  158.6 1.4 fusion.8
  160.0 1.6 fusion.7
  (8 shorter events, 0.1 us)
Async XLA Ops:
  0.0 6.2 %copy-start = (bf16[4096,8]{0,1:T(8,128)(2,1)S(1)}, bf16[4096,8]{0,1:T(8,128)(2,1)}, u32[]{:S(2)}) copy-start(bf16[4096,8]{0,1:T(8,128)(2,1)} %param.11) | copy-start | bytes 196612
  0.0 6.6 %copy-start.3 = (bf16[128,4096]{1,0:T(8,128)(2,1)S(1)}, bf16[128,4096]{1,0:T(8,128)(2,1)}, u32[]{:S(2)}) copy-start(bf16[128,4096]{1,0:T(8,128)(2,1)} %param.9) | copy-start | bytes 3145732
  157.4 1.2 copy-start.1
  157.4 1.2 copy-start.2

commit v3 on v2

--- a/solution.py
+++ b/solution.py
@@ -71,7 +71,9 @@
 
 
 def ordered(step, count):
-    return lax.rem(step, 2) * (count // 2) + lax.div(step, 2)
+    far = lax.div(step + 5, count)
+    late = lax.div(step + 1, count)
+    return step + far - 5 * late
 
 
 def carry(total, width, capacity):
@@ -155,9 +157,8 @@
         )
     pl.semaphore_wait(barrier, count + 1)
 
-    @pl.loop(1, count)
-    def _(step):
-        direct(ordered(step, count)).start()
+    for k in (1, 4, 2):
+        direct(k).start()
 
     def compute(k):
         acc_both[...] = jnp.zeros_like(acc_both)
@@ -224,6 +225,19 @@
         @pl.when(jnp.logical_and(step >= 1, step < count))
         def _():
             direct(ordered(step, count)).wait_recv()
+
+        @pl.when(step == 2)
+        def _():
+            direct(5).start()
+
+        @pl.when(step == 4)
+        def _():
+            direct(6).start()
+
+        @pl.when(step == 5)
+        def _():
+            direct(7).start()
+            direct(3).start()
 
         @stage(step, 0)
         def _():
@@ -363,17 +377,24 @@
             slots.reshape(experts, 2 * capacity, model_width), capacity, w_gate, w_up, w_down
         )
         half = model_width // 2
-        low, high = packed[:, :capacity], packed[:, capacity:]
-        returned = jnp.concatenate([low[:, :, :half], high[:, :, :half]], axis=2)
-        returned = returned.reshape(slot_total, model_width)
-        dots = low[:, :, half].astype(F32) + high[:, :, half].astype(F32)
-        dots = dots.reshape(slot_total)
+        own = (place[:, None] == jnp.arange(2 * slot_total, dtype=jnp.int32)[None, :]).astype(BF16)
+        own_high = (
+            place[:, None] + capacity == jnp.arange(2 * slot_total, dtype=jnp.int32)[None, :]
+        ).astype(BF16)
+        packed = packed.reshape(2 * slot_total, half + LANES)
+        low = jnp.dot(own, packed, preferred_element_type=F32)
+        high = jnp.dot(own_high, packed, preferred_element_type=F32)
+        raw_back = jnp.concatenate([low[:, :half], high[:, :half]], axis=1)
+        gate_grad = low[:, half] + high[:, half]
     else:
         slots_up = pick(target, slot_total, upstream).reshape(experts, capacity, model_width)
         slots_normed = pick(target, slot_total, normed).reshape(experts, capacity, model_width)
         returned, dots = exchange_collective(
             slots_normed, slots_up, w_gate[0], w_up[0], w_down[0]
         )
+        own = target[:, None] == jnp.arange(slot_total, dtype=jnp.int32)[None, :]
+        raw_back = jnp.dot(own.astype(BF16), returned, preferred_element_type=F32)
+        gate_grad = jnp.sum(jnp.where(own, dots[None, :], 0.0), axis=1)
 
     logits = jnp.dot(normed, router, preferred_element_type=F32)
     probability = jax.nn.softmax(logits, axis=1)
@@ -381,9 +402,6 @@
     route_mass = jnp.sum(probability * member, axis=1)
     gate_value = top_prob / route_mass
 
-    own = target[:, None] == jnp.arange(slot_total, dtype=jnp.int32)[None, :]
-    raw_back = jnp.dot(own.astype(BF16), returned, preferred_element_type=F32)
-    gate_grad = jnp.sum(jnp.where(own, dots[None, :], 0.0), axis=1)
     expert_grad = gate_value[:, None] * raw_back
     prob_grad = gate_grad[:, None] * (
         primary / route_mass[:, None] - (top_prob / (route_mass * route_mass))[:, None] * member

time: 162 us -> 146 us (0.901)
  Pallas kernels: 145 us -> 132 us
  other arithmetic: 8.81 us -> 5.01 us
  matrix products: 5.08 us -> 7.33 us
    pallas_call x1, Pallas kernels: 145 us -> 132 us  [exchange_kernel(): pl.pallas_call(functools.partial(exchange_body, count, capacity), out_sha...]
    dot_general x1 -> x2, matrix products: 0.49 us -> 2.61 us  [the longest x1 2.08 us: per_device(): low = jnp.dot(own, packed, preferred_element_type=F32)]
where the time goes in v3:
time: 146 us
  Pallas kernels  132 us (90%)
  matrix products  7.33 us (5%)
  other arithmetic  5.01 us (3%)
    pallas_call x1, Pallas kernels, exchange_kernel(): pl.pallas_call(functools.partial(exchange_body, count, capacity), out_sha...  132 us

profile of v3, /device:TPU:0, one launch (start us, length us, event | category | flops | bytes accessed | tf_op | source)
XLA Modules:
  0.0 145.6 jit_solution(12997824972193131647)
XLA Ops:
  0.0 0.0 copy-start
  0.0 0.0 copy-start.4
  0.0 1.6 %fusion.1 = f32[128]{0:T(128)S(1)} fusion(bf16[128,4096]{1,0:T(8,128)(2,1)} %param.8), kind=kLoop, calls=%fused_computation.7 | loop fusion | flops 1572736 | bytes 1049088 | tf_op jit(solution)/shard_map/reduce_sum | solution.py:365
  1.6 1.6 %fusion.3 = bf16[128,4096]{1,0:T(8,128)(2,1)S(1)} fusion(bf16[128,4096]{1,0:T(8,128)(2,1)} %param.8, f32[4096]{0:T(1024)} %param.10, f32[128]{0:T(128)S(1)} %get-tuple-element.14), kind=kLoop, calls=%fused_computation.9 | loop fusion | flops 2097152 | bytes 2114048 | tf_op jit(solution)/shard_map/convert_element_type | solution.py:366
  3.2 0.0 copy-done
  3.2 0.4 fusion.31
  3.6 0.0 copy-done.4
  3.7 0.1 fusion.12
  3.9 0.0 copy-done.5
  3.9 2.7 %convolution_convert_fusion = bf16[384,4096]{1,0:T(8,128)(2,1)} fusion(bf16[128,4096]{1,0:T(8,128)(2,1)S(1)} %copy-done.5, bf16[128,4096]{1,0:T(8,128)(2,1)S(1)} %fusion.3, s32[256]{0:T(256)S(1)} %pad_add_fusion), kind=kOutput, calls=%fused_computation | convolution fusion | flops 811171840 | bytes 5243904 | tf_op jit(solution)/shard_map/dot_general | solution.py:20
  6.6 131.9 %shard_map.82 = bf16[8,48,2176]{2,1,0:T(8,128)(2,1)} custom-call(bf16[8,48,4096]{2,1,0:T(8,128)(2,1)} %bitcast.40, bf16[1,4096,384]{2,1,0:T(8,128)(2,1)} %gate_hbm.1, bf16[1,4096,384]{2,1,0:T(8,128)(2,1)} %up_hbm.1, bf16[1,384,4096]{2,1,0:T(8,128)(2,1)} %down_hbm.1), custom_call_target="tpu_custom_call" | custom-call | tf_op jit(solution)/shard_map/pallas_call | solution.py:320
  138.5 0.0 copy-start.2
  138.5 2.1 %fusion.14 = f32[128,2176]{1,0:T(8,128)S(1)} fusion(bf16[384,2176]{1,0:T(8,128)(2,1)} %bitcast.38, s32[128]{0:T(128)S(1)} %get-tuple-element.9), kind=kOutput, calls=%fused_computation.25 | convolution fusion | flops 213958656 | bytes 2785792 | tf_op jit(solution)/shard_map/dot_general | solution.py:385
  140.6 0.0 copy-done.2
  140.6 0.5 fusion.15
  141.1 0.1 fusion.18
  141.3 0.0 copy-start.1
  141.3 0.0 copy-start.3
  141.3 0.1 slice.25
  141.4 0.1 slice.26
  141.5 1.0 copy-done.1
  142.5 0.0 copy-done.3
  142.5 1.5 %fusion.8 = (f32[128]{0:T(128)S(1)}, f32[128,4096]{1,0:T(8,128)S(1)}) fusion(bf16[128,4096]{1,0:T(8,128)(2,1)S(1)} %copy-done.1, f32[4096]{0:T(1024)S(1)} %copy-done.3, bf16[4096,8]{0,1:T(8,128)(2,1)S(1)} %copy-done, f32[128]{0:T(128)S(1)} %multiply_reduce_fusion, f32[128,8]{0,1:T(8,128)S(1)} %fusion.20, f32[128]{0:T(128)S(1)} %get-tuple-element.11, ...), kind=kOutput, calls=%fused_computation.14 | convolution fusion | flops 54009728 | bytes 5341184 | tf_op jit(solution)/shard_map/dot_general | solution.py:410
  144.0 1.6 %fusion.7 = bf16[128,4096]{1,0:T(8,128)(2,1)} fusion(bf16[128,4096]{1,0:T(8,128)(2,1)S(1)} %copy-done.1, f32[128,4096]{1,0:T(8,128)S(1)} %get-tuple-element.18, f32[128]{0:T(128)S(1)} %get-tuple-element.17, f32[128]{0:T(128)S(1)} %get-tuple-element.13, f32[128]{0:T(128)S(1)} %get-tuple-element.14), kind=kLoop, calls=%fused_computation.13 | loop fusion | flops 3670016 | bytes 4195840 | tf_op jit(solution)/shard_map/convert_element_type | solution.py:418
  (11 shorter events, 0.2 us)
Async XLA Ops:
  0.0 3.2 %copy-start = (bf16[4096,8]{0,1:T(8,128)(2,1)S(1)}, bf16[4096,8]{0,1:T(8,128)(2,1)}, u32[]{:S(2)}) copy-start(bf16[4096,8]{0,1:T(8,128)(2,1)} %param.11) | copy-start | bytes 196612
  0.0 3.6 %copy-start.4 = (s32[128,8]{0,1:T(8,128)S(1)}, s32[128,8]{0,1:T(8,128)}, u32[]{:S(2)}) copy-start(s32[128,8]{0,1:T(8,128)} %param.12) | copy-start | bytes 12292
  0.0 3.9 %copy-start.5 = (bf16[128,4096]{1,0:T(8,128)(2,1)S(1)}, bf16[128,4096]{1,0:T(8,128)(2,1)}, u32[]{:S(2)}) copy-start(bf16[128,4096]{1,0:T(8,128)(2,1)} %param.9) | copy-start | bytes 3145732
  138.5 2.1 %copy-start.2 = (bf16[8,48,2176]{2,1,0:T(8,128)(2,1)S(1)}, bf16[8,48,2176]{2,1,0:T(8,128)(2,1)}, u32[]{:S(2)}) copy-start(bf16[8,48,2176]{2,1,0:T(8,128)(2,1)} %shard_map.82) | copy-start | bytes 5013508
  141.3 1.2 copy-start.1
  141.3 1.2 copy-start.3
